TPU v7x, 32 devices: a whole 2x2x4 slice. The times are simulated.
32 devices in a mesh: dp: 2 (over core), row: 4 (over y, x), col: 4 (over z).
Axes of the slice: x: 2, y: 2, z: 4, core: 2. Of those that a mesh axis runs over, the one named last changes fastest.
Arguments:
- tokens: bfloat16 [1024, 768], P(('dp', 'col'), 'row'), may hold values from -150 to 150
- out_grad: bfloat16 [1024, 768], P(('dp', 'col'), 'row'), may hold values from -6 to 6
- segment_ids: int32 [2, 512], P('dp'), may hold values from 0 to 1, never falling along the last dimension, each value on 1 to 384 neighbouring positions
- w_qkv: bfloat16 [768, 2304], P('row', 'col'), may hold values from -8 to 8
- w_out: bfloat16 [768, 768], P('col', 'row'), may hold values from -0.875 to 0.875
- w_fc: bfloat16 [768, 3072], P('row', 'col'), may hold values from -0.21875 to 0.21875
- w_proj: bfloat16 [3072, 768], P('col', 'row'), may hold values from -0.109375 to 0.109375
- bias_qkv: float32 [2304], P('col'), may hold values from -1.8 to 1.8
- bias_fc: float32 [3072], P('col'), may hold values from -1.8 to 1.8
- row_vectors: float32 [6, 768], P(None, 'row'), may hold values from -0.6 to 1.5
- mom_qkv: float32 [768, 2304], P('row', 'col'), may hold values from -20 to 20
- mom_out: float32 [768, 768], P('col', 'row'), may hold values from -20 to 20
- mom_fc: float32 [768, 3072], P('row', 'col'), may hold values from -20 to 20
- mom_proj: float32 [3072, 768], P('col', 'row'), may hold values from -20 to 20
- mom_bias_qkv: float32 [2304], P('col'), may hold values from -20 to 20
- mom_bias_fc: float32 [3072], P('col'), may hold values from -20 to 20
- mom_rows: float32 [6, 768], P(None, 'row'), may hold values from -20 to 20
Outputs:
- block_out: bfloat16 [1024, 768], P(('dp', 'col'), 'row')
- input_grad: float32 [1024, 768], P(('dp', 'col'), 'row')
- grad_qkv: float32 [768, 2304], P('row', 'col')
- grad_out: float32 [768, 768], P('col', 'row')
- grad_fc: float32 [768, 3072], P('row', 'col')
- grad_proj: float32 [3072, 768], P('col', 'row')
- grad_bias_qkv: float32 [2304], P('col')
- grad_bias_fc: float32 [3072], P('col')
- grad_rows: float32 [6, 768], P(None, 'row')
- new_qkv: float32 [768, 2304], P('row', 'col')
- new_out: float32 [768, 768], P('col', 'row')
- new_fc: float32 [768, 3072], P('row', 'col')
- new_proj: float32 [3072, 768], P('col', 'row')
- new_bias_qkv: float32 [2304], P('col')
- new_bias_fc: float32 [3072], P('col')
- new_rows: float32 [6, 768], P(None, 'row')
- new_mom_qkv: float32 [768, 2304], P('row', 'col')
- new_mom_out: float32 [768, 768], P('col', 'row')
- new_mom_fc: float32 [768, 3072], P('row', 'col')
- new_mom_proj: float32 [3072, 768], P('col', 'row')
- new_mom_bias_qkv: float32 [2304], P('col')
- new_mom_bias_fc: float32 [3072], P('col')
- new_mom_rows: float32 [6, 768], P(None, 'row')
Inputs may be any that keep to these rules, and one draw needn't show every extreme that they name: `segment_ids`: within each data group the segment numbers never fall; the group's 2 sequences have 512 tokens together, each at most 384.
All inputs are finite; a program needn't handle non-finite values.
Results may differ from a plain program's by a relative error of at most 0.012.
Values may be sent and summed in bfloat16 or wider, within the bound.
A program may use at most 128 MiB of HBM per device.

v0:
```python
import math
import jax
import jax.numpy as jnp
from jax import lax
from jax.sharding import PartitionSpec as P

HD = 64
NS_STEPS = 2
eps_norm = 1e-05
eps_gram = 1e-06
coef_a = 3.4445
coef_b = -4.775
coef_c = 2.0315
beta_mom = 0.95
rate_matrix = 0.03
rate_vector = 0.6


def gelu_value(values):
    return jax.nn.gelu(values, approximate=True)


def gelu_slope(values):
    return jax.vjp(gelu_value, values)[1](jnp.ones_like(values))[0]


def product(left_side, right_side, flip_right):
    if flip_right:
        return lax.dot_general(
            left_side, right_side, (((1,), (1,)), ((), ())), preferred_element_type=jnp.float32
        )
    return jnp.dot(left_side, right_side, preferred_element_type=jnp.float32)


def inner_rows(left_side, right_side):
    return lax.dot_general(
        left_side, right_side, (((0,), (0,)), ((), ())), preferred_element_type=jnp.float32
    )


def tile_grid(blocks, first_parts, second_parts):
    height = blocks.shape[1]
    breadth = blocks.shape[2]
    tiled = blocks.reshape(first_parts, second_parts, height, breadth)
    return tiled.transpose(0, 2, 1, 3).reshape(first_parts * height, second_parts * breadth)


def gather_grid(local_piece):
    blocks = lax.all_gather(local_piece, ("col", "row"), axis=0, tiled=False)
    return tile_grid(
        blocks.reshape((-1,) + local_piece.shape), lax.axis_size("col"), lax.axis_size("row")
    )


def norm_stats(values):
    mean_row = jnp.mean(values, axis=1, keepdims=True)
    square = jnp.mean(values * values, axis=1, keepdims=True)
    inv_std = lax.rsqrt(square - mean_row * mean_row + eps_norm)
    return (mean_row, inv_std)


def matrix_product(left_side, right_side):
    return jnp.dot(
        left_side.astype(jnp.bfloat16),
        right_side.astype(jnp.bfloat16),
        preferred_element_type=jnp.float32,
    )


def polynomial_factor(gram_matrix):
    gram_norm = jnp.sqrt(jnp.sum(gram_matrix * gram_matrix)) + eps_gram
    gram_now = gram_matrix / gram_norm
    poly_before = None
    for repeat in range(NS_STEPS):
        poly = coef_b * gram_now + coef_c * matrix_product(gram_now, gram_now)
        if poly_before is None:
            factor = poly
            scale = coef_a
        else:
            factor = coef_a * factor + scale * poly + matrix_product(poly, factor)
            scale = scale * coef_a
        if repeat + 1 < NS_STEPS:
            half = coef_a * gram_now + matrix_product(poly, gram_now)
            gram_now = coef_a * half + matrix_product(half, poly)
        poly_before = poly
    return (factor, scale, gram_norm)


def local(
    tokens,
    out_grad,
    segment_ids,
    w_qkv,
    w_out,
    w_fc,
    w_proj,
    bias_qkv,
    bias_fc,
    row_vectors,
    mom_qkv,
    mom_out,
    mom_fc,
    mom_proj,
    mom_bias_qkv,
    mom_bias_fc,
    mom_rows,
):
    low = jnp.bfloat16
    score_scale = 1.0 / math.sqrt(HD)
    row_parts = lax.axis_size("row")
    col_parts = lax.axis_size("col")
    dp_parts = lax.axis_size("dp")
    own_tokens, own_features = tokens.shape
    token_count = own_tokens * col_parts
    feature_count = own_features * row_parts
    token_base = lax.axis_index("col") * own_tokens
    feature_base = lax.axis_index("row") * own_features

    def own_columns(whole):
        return lax.dynamic_slice_in_dim(whole, feature_base, own_features, 1)

    def own_block(whole):
        return lax.dynamic_slice(whole, (token_base, feature_base), (own_tokens, own_features))

    def own_rows(whole):
        return lax.dynamic_slice_in_dim(whole, token_base, own_tokens, 0)

    tokens_all = gather_grid(tokens)
    qkv_cols = lax.all_gather(w_qkv, "row", axis=0, tiled=True)
    vectors_all = lax.all_gather(row_vectors, "row", axis=1, tiled=True)
    out_whole = gather_grid(w_out)
    fc_cols = lax.all_gather(w_fc, "row", axis=0, tiled=True)
    grad_all = gather_grid(out_grad)
    proj_flip = w_proj.T
    proj_cols = lax.all_gather(proj_flip, "row", axis=0, tiled=True)
    gain_one, shift_one, gain_two, shift_two, bias_out, _ = [
        vectors_all[which] for which in range(6)
    ]
    resid_in = tokens_all.astype(jnp.float32)
    mean_one, inv_one = norm_stats(resid_in)
    unit_one = (resid_in - mean_one) * inv_one
    act_one = (unit_one * gain_one + shift_one).astype(low)
    qkv_local = (product(act_one, qkv_cols, False) + bias_qkv).astype(low)
    heads_local = qkv_local.shape[1] // (3 * HD)
    qkv_tiles = qkv_local.reshape(token_count, heads_local, 3, HD).transpose(2, 1, 0, 3)
    query, key, value = (qkv_tiles[0], qkv_tiles[1], qkv_tiles[2])
    segment_row = segment_ids[0]
    positions = jnp.arange(token_count, dtype=jnp.int32)
    allowed = (positions[None, :] <= positions[:, None]) & (
        segment_row[None, :] == segment_row[:, None]
    )
    scores = (
        jnp.einsum("hqe,hke->hqk", query, key, preferred_element_type=jnp.float32) * score_scale
    )
    scores = jnp.where(allowed[None], scores, -jnp.inf)
    row_max = jnp.max(scores, axis=2, keepdims=True)
    raised = jnp.exp(scores - row_max)
    probs = raised / jnp.sum(raised, axis=2, keepdims=True)
    prob_low = probs.astype(low)
    attended = jnp.einsum(
        "hqk,hke->hqe", prob_low, value, preferred_element_type=jnp.float32
    ).astype(low)
    attn_local = attended.transpose(1, 0, 2).reshape(token_count, heads_local * HD)
    attn_all = lax.all_gather(attn_local, "col", axis=1, tiled=True)
    resid_mid = resid_in + product(attn_all, out_whole, False) + bias_out
    mean_two, inv_two = norm_stats(resid_mid)
    unit_two = (resid_mid - mean_two) * inv_two
    act_two = (unit_two * gain_two + shift_two).astype(low)
    hidden_pre = product(act_two, fc_cols, False) + bias_fc
    hidden = gelu_value(hidden_pre).astype(low)
    grad_hidden = product(grad_all, proj_cols, False)
    grad_pre = (gelu_slope(hidden_pre) * grad_hidden).astype(low)
    grad_norm_two = lax.psum_scatter(
        product(grad_pre, w_fc, True).astype(low), "col", scatter_dimension=0, tiled=True
    )
    grad_two_all = gather_grid(grad_norm_two).astype(jnp.float32)
    grad_norm_two = grad_norm_two.astype(jnp.float32)
    scaled = grad_two_all * gain_two
    first_mean = jnp.mean(scaled, axis=1, keepdims=True)
    second_mean = jnp.mean(scaled * unit_two, axis=1, keepdims=True)
    grad_mid_all = grad_all.astype(jnp.float32) + inv_two * (
        scaled - first_mean - unit_two * second_mean
    )
    grad_mid_low = grad_mid_all.astype(low)
    out_rows = lax.dynamic_slice_in_dim(
        out_whole, lax.axis_index("col") * w_out.shape[0], w_out.shape[0], 0
    )
    grad_attn = (
        product(grad_mid_low, out_rows, True)
        .astype(low)
        .reshape(token_count, heads_local, HD)
        .transpose(1, 0, 2)
    )
    grad_value = jnp.einsum("hqk,hqe->hke", prob_low, grad_attn, preferred_element_type=jnp.float32)
    grad_probs = jnp.einsum("hqe,hke->hqk", grad_attn, value, preferred_element_type=jnp.float32)
    row_dot = jnp.sum(
        grad_attn.astype(jnp.float32) * attended.astype(jnp.float32), axis=2, keepdims=True
    )
    grad_scores = (score_scale * probs * (grad_probs - row_dot)).astype(low)
    grad_query = jnp.einsum("hqk,hke->hqe", grad_scores, key, preferred_element_type=jnp.float32)
    grad_key = jnp.einsum("hqk,hqe->hke", grad_scores, query, preferred_element_type=jnp.float32)
    grad_qkv_low = (
        jnp.stack([grad_query.astype(low), grad_key.astype(low), grad_value.astype(low)], axis=0)
        .transpose(2, 1, 0, 3)
        .reshape(token_count, heads_local * 3 * HD)
    )
    grad_blocks = (
        inner_rows(own_columns(act_one), grad_qkv_low),
        inner_rows(attn_local, own_columns(grad_mid_low)),
        inner_rows(own_columns(act_two), grad_pre),
        inner_rows(hidden, own_columns(grad_all)),
    )
    summed = [lax.psum(block.astype(low), "dp").astype(jnp.float32) for block in grad_blocks]
    bias_sums = lax.psum(
        (
            jnp.sum(grad_qkv_low, axis=0, dtype=jnp.float32),
            jnp.sum(grad_pre, axis=0, dtype=jnp.float32),
        ),
        "dp",
    )
    summed = summed + list(bias_sums)
    weights = (w_qkv, w_out, w_fc, w_proj)
    moments = (mom_qkv, mom_out, mom_fc, mom_proj)
    flips = (False, True, False, True)
    new_moms = [beta_mom * moments[member] + summed[member] for member in range(4)]
    pushes = [(summed[member] + beta_mom * new_moms[member]).astype(low) for member in range(4)]
    upright = [pushes[member].T if flips[member] else pushes[member] for member in range(4)]
    widest = max((piece.shape[1] for piece in upright))
    share = -(-widest // dp_parts)
    assert row_parts == len(upright)
    outgoing = jnp.stack(
        [jnp.pad(piece, ((0, 0), (0, share * dp_parts - piece.shape[1]))) for piece in upright]
    )
    outgoing = lax.dynamic_slice_in_dim(outgoing, lax.axis_index("dp") * share, share, 2)
    arrived = lax.all_to_all(outgoing, "row", split_axis=0, concat_axis=0, tiled=True)
    matrix = arrived.reshape(feature_count, share)
    gram = lax.psum(product(matrix, matrix, True).astype(low), ("dp", "col")).astype(jnp.float32)
    factor, scale, gram_norm = polynomial_factor(gram)
    ortho = (scale * matrix.astype(jnp.float32) + matrix_product(factor, matrix)) * lax.rsqrt(
        gram_norm
    )
    back = lax.all_to_all(
        ortho.astype(low).reshape(row_parts, own_features, share),
        "row",
        split_axis=0,
        concat_axis=0,
        tiled=True,
    )
    orthos = lax.all_gather(back, "dp", axis=2, tiled=True)
    new_weights = []
    for member in range(4):
        piece = orthos[member, :, : upright[member].shape[1]]
        if flips[member]:
            piece = piece.T
        longest = max(upright[member].shape[0] * row_parts, upright[member].shape[1] * col_parts)
        new_weights.append(
            weights[member].astype(jnp.float32)
            - rate_matrix * math.sqrt(longest) * piece.astype(jnp.float32)
        )
    block_sum = lax.psum_scatter(
        product(hidden, proj_flip, True).astype(low), "col", scatter_dimension=0, tiled=True
    ).astype(jnp.float32)
    block_out = (own_block(resid_mid) + block_sum + row_vectors[5]).astype(low)
    grad_norm_one = lax.psum_scatter(
        product(grad_qkv_low, w_qkv, True).astype(low), "col", scatter_dimension=0, tiled=True
    ).astype(jnp.float32)
    unit_one_own = own_block(unit_one)
    scaled_one = grad_norm_one * row_vectors[0]
    first_sum, second_sum = lax.psum(
        (
            jnp.sum(scaled_one, axis=1, keepdims=True),
            jnp.sum(scaled_one * unit_one_own, axis=1, keepdims=True),
        ),
        "row",
    )
    input_grad = own_block(grad_mid_all) + own_rows(inv_one) * (
        scaled_one - first_sum / feature_count - unit_one_own * (second_sum / feature_count)
    )
    row_terms = jnp.stack(
        [
            jnp.sum(grad_norm_one * unit_one_own, axis=0),
            jnp.sum(grad_norm_one, axis=0),
            jnp.sum(grad_norm_two * own_block(unit_two), axis=0),
            jnp.sum(grad_norm_two, axis=0),
            jnp.sum(own_block(grad_mid_low), axis=0, dtype=jnp.float32),
            jnp.sum(out_grad, axis=0, dtype=jnp.float32),
        ]
    )
    grad_rows = lax.psum(row_terms, ("dp", "col"))
    vector_rate = rate_vector / math.sqrt(token_count * dp_parts)

    def vector_step(weight, gradient, moment):
        new_moment = beta_mom * moment + gradient
        return (weight - vector_rate * (gradient + beta_mom * new_moment), new_moment)

    new_bias_qkv, new_mom_bias_qkv = vector_step(bias_qkv, summed[4], mom_bias_qkv)
    new_bias_fc, new_mom_bias_fc = vector_step(bias_fc, summed[5], mom_bias_fc)
    new_rows, new_mom_rows = vector_step(row_vectors, grad_rows, mom_rows)
    return (
        block_out,
        input_grad,
        summed[0],
        summed[1],
        summed[2],
        summed[3],
        summed[4],
        summed[5],
        grad_rows,
        new_weights[0],
        new_weights[1],
        new_weights[2],
        new_weights[3],
        new_bias_qkv,
        new_bias_fc,
        new_rows,
        new_moms[0],
        new_moms[1],
        new_moms[2],
        new_moms[3],
        new_mom_bias_qkv,
        new_mom_bias_fc,
        new_mom_rows,
    )


def solution(mesh):
    placed = (
        P(("dp", "col"), "row"),
        P(("dp", "col"), "row"),
        P("dp", None),
        P("row", "col"),
        P("col", "row"),
        P("row", "col"),
        P("col", "row"),
        P("col"),
        P("col"),
        P(None, "row"),
        P("row", "col"),
        P("col", "row"),
        P("row", "col"),
        P("col", "row"),
        P("col"),
        P("col"),
        P(None, "row"),
    )
    return jax.shard_map(
        local,
        mesh=mesh,
        in_specs=placed,
        out_specs=(
            P(("dp", "col"), "row"),
            P(("dp", "col"), "row"),
            P("row", "col"),
            P("col", "row"),
            P("row", "col"),
            P("col", "row"),
            P("col"),
            P("col"),
            P(None, "row"),
            P("row", "col"),
            P("col", "row"),
            P("row", "col"),
            P("col", "row"),
            P("col"),
            P("col"),
            P(None, "row"),
            P("row", "col"),
            P("col", "row"),
            P("row", "col"),
            P("col", "row"),
            P("col"),
            P("col"),
            P(None, "row"),
        ),
        check_vma=False,
    )
```

profile of v0, /device:TPU:0, one launch (start us, length us, event | category | flops | bytes accessed | tf_op | source)
XLA Modules:
  0.0 442.9 jit_solution(18156364736476720442)
XLA Ops:
  9.5 47.6 %all-gather = bf16[2048,192]{0,1:T(8,128)(2,1)S(1)} all-gather(bf16[128,192]{0,1:T(8,128)(2,1)} %param.17), channel_id=2, replica_groups=mesh['dp'=2,'row'=4,'col'=4] {'col','row'}, dimensions={0}, use_global_device_ids=true | all-gather | bytes 835584 | tf_op jit(solution)/shard_map/all_gather | solution.py:49
  60.2 6.9 %all-gather.4 = f32[4,192,6]{1,2,0:T(8,128)S(1)} all-gather(f32[1,192,6]{1,2,0:T(8,128)S(1)} %bitcast.210), channel_id=1, replica_groups=mesh['dp'=2,'row'=4,'col'=4] {'row'}, dimensions={0}, use_global_device_ids=true | all-gather | bytes 23040 | tf_op jit(solution)/shard_map/all_gather | solution.py:130
  69.0 13.3 %all_gather.45 = bf16[768,576]{1,0:T(8,128)(2,1)S(1)} all-gather(bf16[192,576]{1,0:T(8,128)(2,1)S(1)} %copy-done.16), channel_id=1, replica_groups=mesh['dp'=2,'row'=4,'col'=4] {'row'}, dimensions={0}, use_global_device_ids=true | all-gather | bytes 1105920 | tf_op jit(solution)/shard_map/all_gather | solution.py:129
  85.5 43.6 %all-gather.2 = bf16[2048,192]{0,1:T(8,128)(2,1)S(1)} all-gather(bf16[128,192]{0,1:T(8,128)(2,1)S(1)} %copy-done.30), channel_id=4, replica_groups=mesh['dp'=2,'row'=4,'col'=4] {'col','row'}, dimensions={0}, use_global_device_ids=true | all-gather | bytes 835584 | tf_op jit(solution)/shard_map/all_gather | solution.py:49
  131.5 4.1 fusion.73
  139.4 16.6 %all_gather.46 = bf16[512,768]{0,1:T(8,128)(2,1)} all-gather(bf16[512,192]{0,1:T(8,128)(2,1)S(1)} %bitcast.195), channel_id=1, replica_groups=mesh['dp'=2,'row'=4,'col'=4] {'col'}, dimensions={1}, use_global_device_ids=true | all-gather | bytes 983040 | tf_op jit(solution)/shard_map/all_gather | solution.py:164
  156.0 3.9 copy.219
  159.9 3.1 reshape.253
  163.0 2.6 fusion.70
  168.0 3.8 multiply_convert_fusion.1
  171.9 4.2 convert_reduce_fusion
  182.8 12.3 %reduce-scatter.12.cloned.1.call-done = bf16[128,192]{1,0:T(8,128)(2,1)} async-done(((bf16[512,192]{1,0:T(8,128)(2,1)}), bf16[128,192]{1,0:T(8,128)(2,1)}) %reduce-scatter.12.cloned.1.call-update) | async-done | bytes 49168 | tf_op jit(solution)/shard_map/reduce_scatter | solution.py:173
  196.0 44.7 %all-gather.3 = bf16[2048,192]{0,1:T(8,128)(2,1)} all-gather(bf16[128,192]{0,1:T(8,128)(2,1)S(1)} %copy.201), channel_id=5, replica_groups=mesh['dp'=2,'row'=4,'col'=4] {'col','row'}, dimensions={0}, use_global_device_ids=true | all-gather | bytes 835584 | tf_op jit(solution)/shard_map/all_gather | solution.py:49
  244.7 3.1 copy.174
  260.4 15.7 %all-reduce.10.cloned.1.call-done = (bf16[192,192]{0,1:T(8,128)(2,1)}, bf16[192,576]{1,0:T(8,128)(2,1)}, bf16[192,768]{1,0:T(8,128)(2,1)}, bf16[768,192]{0,1:T(8,128)(2,1)}) async-done(((bf16[192,192]{0,1:T(8,128)(2,1)}, bf16[192,576]{1,0:T(8,128)(2,1)}, bf16[192,768]{1,0:T(8,128)(2,1)}, bf16[768,192]{0,1:T(8,128)(2,1)}), (bf16[192,192]{0,1:T(8,128)(2,1)}, bf16[192,576]{1,0:T(8,128)(2,1)}, ...) | async-done | bytes 884752 | tf_op jit(solution)/shard_map/psum | solution.py:213
  281.7 13.6 %all_to_all.10 = bf16[4,192,384]{2,1,0:T(8,128)(2,1)S(1)} all-to-all(bf16[4,192,384]{2,1,0:T(8,128)(2,1)S(1)} %fusion.34), channel_id=1, replica_groups=mesh['dp'=2,'row'=4,'col'=4] {'row'}, dimensions={0} | all-to-all | bytes 1179648 | tf_op jit(solution)/shard_map/all_to_all | solution.py:235
  305.9 50.5 %all-reduce.8.cloned.1.call-done = bf16[768,768]{1,0:T(8,128)(2,1)} async-done(((bf16[768,768]{1,0:T(8,128)(2,1)}), bf16[768,768]{1,0:T(8,128)(2,1)}) %all-reduce.8.cloned.1.call-update) | async-done | bytes 1179664 | tf_op jit(solution)/shard_map/psum | solution.py:237
  359.6 3.4 multiply_add_fusion.4
  368.1 6.3 %fusion.18 = bf16[768,384]{1,0:T(8,128)(2,1)} fusion(bf16[768,384]{1,0:T(8,128)(2,1)S(1)} %bitcast.188, f32[768,768]{1,0:T(8,128)} %copy-done.13, f32[768,768]{1,0:T(8,128)} %multiply_add_fusion.1, f32[]{:T(128)S(6)} %rsqrt.28), kind=kOutput, calls=%fused_computation.51 | convolution fusion | flops 1363968000 | bytes 5898244 | tf_op jit(solution)/shard_map/dot_general | solution.py:63
  374.5 3.8 all-to-all-start.1
  381.0 2.6 all-reduce.3
  388.3 11.0 %reduce-scatter.14.cloned.1.call-done = bf16[128,192]{1,0:T(8,128)(2,1)} async-done(((bf16[512,192]{1,0:T(8,128)(2,1)}), bf16[128,192]{1,0:T(8,128)(2,1)}) %reduce-scatter.14.cloned.1.call-update) | async-done | bytes 49168 | tf_op jit(solution)/shard_map/reduce_scatter | solution.py:264
  400.5 9.9 %all-reduce.2 = (f32[128,1]{0,1:T(1,128)S(1)}, f32[128,1]{0,1:T(1,128)S(1)}) all-reduce(f32[128,1]{0,1:T(1,128)S(1)} %bitcast.222, f32[128,1]{0,1:T(1,128)S(1)} %bitcast.223), channel_id=1, replica_groups=mesh['dp'=2,'row'=4,'col'=4] {'row'}, use_global_device_ids=true, to_apply=%region_15.16 | all-reduce | flops 256 | bytes 2048 | tf_op jit(solution)/shard_map/psum | solution.py:269
  412.4 14.4 %psum.78 = f32[6,192]{1,0:T(8,128)S(1)} all-reduce(f32[6,192]{1,0:T(8,128)S(1)} %stack.58), channel_id=1, replica_groups=mesh['dp'=2,'row'=4,'col'=4] {'dp','col'}, use_global_device_ids=true, to_apply=%region_30.31 | all-reduce | flops 1152 | bytes 9216 | tf_op jit(solution)/shard_map/psum | solution.py:289
  (202 shorter events, 86.7 us)
Async XLA Ops:
  7.2 148.8 %all-gather.16.cloned.1.call-start = ((), (), s32[]{:S(2)}) async-start(), calls=%async_computation.9 | async-start | bytes 1671168 | tf_op jit(solution)/shard_map/all_gather | solution.py:49
  7.9 160.1 %all-gather.10.cloned.1.call-start = ((), (), s32[]{:S(2)}) async-start(), calls=%async_computation.5 | async-start | bytes 1474560 | tf_op jit(solution)/shard_map/all_gather | solution.py:132
  8.7 163.2 %all-gather.12.cloned.1.call-start = ((), (), s32[]{:S(2)}) async-start(), calls=%async_computation.6 | async-start | bytes 1474560 | tf_op jit(solution)/shard_map/all_gather | solution.py:135
  9.4 185.6 %reduce-scatter.12.cloned.1.call-start = ((), (), s32[]{:S(2)}) async-start(), calls=%async_computation.11 | async-start | bytes 327680 | tf_op jit(solution)/shard_map/reduce_scatter | solution.py:173
  137.9 22.0 %copy-start.1 = (bf16[3,512,512]{1,2,0:T(8,128)(2,1)}, bf16[3,512,512]{1,2,0:T(8,128)(2,1)S(1)}, u32[]{:S(2)}) copy-start(bf16[3,512,512]{1,2,0:T(8,128)(2,1)S(1)} %fusion.19) | copy-start | bytes 4718596
  178.3 97.8 %all-reduce.10.cloned.1.call-start = ((), (), s32[]{:S(2)}) async-start(), calls=%async_computation.13 | async-start | bytes 1867776 | tf_op jit(solution)/shard_map/psum | solution.py:213
  260.2 96.2 %all-reduce.8.cloned.1.call-start = ((), (), s32[]{:S(2)}) async-start(), calls=%async_computation.7 | async-start | bytes 2359296 | tf_op jit(solution)/shard_map/psum | solution.py:237
  297.1 86.5 %reduce-scatter.10.cloned.1.call-start = ((), (), s32[]{:S(2)}) async-start(), calls=%async_computation.10 | async-start | bytes 327680 | tf_op jit(solution)/shard_map/reduce_scatter | solution.py:260
  301.2 98.1 %reduce-scatter.14.cloned.1.call-start = ((), (), s32[]{:S(2)}) async-start(), calls=%async_computation.12 | async-start | bytes 327680 | tf_op jit(solution)/shard_map/reduce_scatter | solution.py:264
  374.4 11.7 %copy-start.38 = (f32[576]{0:T(1024)S(1)}, f32[576]{0:T(1024)}, u32[]{:S(2)}) copy-start(f32[576]{0:T(1024)} %param.24) | copy-start | bytes 6916
  374.4 11.7 %copy-start.39 = (f32[576]{0:T(1024)S(1)}, f32[576]{0:T(1024)}, u32[]{:S(2)}) copy-start(f32[576]{0:T(1024)} %param.31) | copy-start | bytes 6916
  374.4 13.1 %copy-start.29 = (bf16[128,192]{1,0:T(8,128)(2,1)S(1)}, bf16[128,192]{1,0:T(8,128)(2,1)}, u32[]{:S(2)}) copy-start(bf16[128,192]{1,0:T(8,128)(2,1)} %reduce-scatter.12.cloned.1.call-done) | copy-start | bytes 147460
  374.4 13.3 %copy-start.41 = (f32[768]{0:T(1024)S(1)}, f32[768]{0:T(1024)}, u32[]{:S(2)}) copy-start(f32[768]{0:T(1024)} %param.25) | copy-start | bytes 9220
  374.4 13.3 %copy-start.42 = (f32[768]{0:T(1024)S(1)}, f32[768]{0:T(1024)}, u32[]{:S(2)}) copy-start(f32[768]{0:T(1024)} %param.32) | copy-start | bytes 9220
  374.5 24.9 %copy-start.34 = (f32[1,192]{1,0:T(1,128)S(1)}, f32[1,192]{1,0:T(1,128)}, u32[]{:S(2)}) copy-start(f32[1,192]{1,0:T(1,128)} %get-tuple-element.209) | copy-start | bytes 2308
  374.5 52.4 %copy-start.36 = (f32[6,192]{1,0:T(8,128)S(1)}, f32[6,192]{1,0:T(8,128)}, u32[]{:S(2)}) copy-start(f32[6,192]{1,0:T(8,128)} %param.33) | copy-start | bytes 13828
  374.5 10.8 %all-to-all-start.1 = ((bf16[4,192,384]{2,1,0:T(8,128)(2,1)}), bf16[4,192,384]{2,1,0:T(8,128)(2,1)S(1)}, u32[]{:S(2)}, u32[]{:S(2)}) async-start(bf16[4,192,384]{2,1,0:T(8,128)(2,1)} %bitcast.207), calls=%async_computation.1 | async-start | bytes 1179648 | tf_op jit(solution)/shard_map/all_to_all | solution.py:242
  378.2 49.2 %copy-start.26 = (bf16[192,192]{0,1:T(8,128)(2,1)S(1)}, bf16[192,192]{0,1:T(8,128)(2,1)}, u32[]{:S(2)}) copy-start(bf16[192,192]{0,1:T(8,128)(2,1)} %get-tuple-element.180) | copy-start | bytes 221188
  378.3 50.0 %copy-start.22 = (f32[192,192]{0,1:T(8,128)S(1)}, f32[192,192]{0,1:T(8,128)}, u32[]{:S(2)}) copy-start(f32[192,192]{0,1:T(8,128)} %get-tuple-element.207) | copy-start | bytes 442372
  378.3 50.8 %all-gather.14.cloned.1.call-start = ((), (), s32[]{:S(2)}) async-start(), calls=%async_computation.8 | async-start | bytes 1769472 | tf_op jit(solution)/shard_map/all_gather | solution.py:249
  383.6 46.4 %copy-start.43 = (f32[576]{0:T(1024)}, f32[576]{0:T(1024)S(1)}, u32[]{:S(2)}) copy-start(f32[576]{0:T(1024)S(1)} %get-tuple-element.178) | copy-start | bytes 6916
  383.6 46.4 %copy-start.44 = (f32[768]{0:T(1024)}, f32[768]{0:T(1024)S(1)}, u32[]{:S(2)}) copy-start(f32[768]{0:T(1024)S(1)} %get-tuple-element.179) | copy-start | bytes 9220
  386.1 44.7 %copy-start.17 = (bf16[192,576]{1,0:T(8,128)(2,1)S(1)}, bf16[192,576]{1,0:T(8,128)(2,1)}, u32[]{:S(2)}) copy-start(bf16[192,576]{1,0:T(8,128)(2,1)} %param.20) | copy-start | bytes 663556
  410.4 22.2 %copy-start.11 = (bf16[192,768]{1,0:T(8,128)(2,1)S(1)}, bf16[192,768]{1,0:T(8,128)(2,1)}, u32[]{:S(2)}) copy-start(bf16[192,768]{1,0:T(8,128)(2,1)} %param.22) | copy-start | bytes 884740
  (31 other events, 81.7 us)
Sparse Core Ops, SparseCore 0:
  10.8 64.3 all-gather.15
  77.0 32.6 all-gather.9
  111.6 27.0 all-gather.11
  178.4 16.5 reduce-scatter.11
  260.3 15.7 all-reduce.9
  297.2 59.0 all-reduce.7
  359.2 19.0 reduce-scatter.9
  381.1 18.2 reduce-scatter.13
  401.5 7.4 all-gather.13
where the time goes:
time: 444 us; the launch traced here: 443 us
  blocking collectives  213 us (48%)
  waiting for transfers between devices  92.2 us (21%)
  matrix products  49.5 us (11%)
  local copies, waits for them, and re-layouts  36.4 us (8%)
  other arithmetic  32 us (7%)
  between operations  15.2 us (3%)
    all_gather x3, blocking collectives, gather_grid(): blocks = lax.all_gather(local_piece, ('col', 'row'), axis=0, tiled=False)  136 us
    psum x1, waiting for transfers between devices, local(): lax.psum(product(matrix, matrix, True).astype(low), ('dp', 'col'))  50.5 us
    unnamed x105, local copies, waits for them, and re-layouts  16.8 us
    all_gather x1, blocking collectives, local(): attn_all = lax.all_gather(attn_local, 'col', axis=1, tiled=True)  16.6 us
    psum x1, waiting for transfers between devices, local(): lax.psum(block.astype(low), 'dp').astype(jnp.float32)  15.7 us
    dot_general x5, matrix products, matrix_product(): jnp.dot(left_side.astype(jnp.bfloat16), right_side.astype(jnp.bfloat16),...  14.5 us
    psum x1, blocking collectives, local(): grad_rows = lax.psum(row_terms, ('dp', 'col'))  14.4 us
    all_to_all x1, blocking collectives, local(): lax.all_to_all(outgoing, 'row', split_axis=0, concat_axis=0, tiled=True)  13.6 us
  transfers between devices with their start and end apart: 10, of which 5 were waited for; matrix products, arithmetic and copies ran while one was open for 17% of the time, Pallas kernels for 0%

commit v1 on v0

--- a/solution.py
+++ b/solution.py
@@ -14,6 +14,12 @@
 beta_mom = 0.95
 rate_matrix = 0.03
 rate_vector = 0.6
+
+
+def _group_steps_all(payload, ax_name):
+    wide_out = lax.all_gather(payload, ax_name)
+    reply = jnp.sum(wide_out, axis=0)
+    return reply
 
 
 def gelu_value(values):
@@ -234,7 +240,9 @@
     outgoing = lax.dynamic_slice_in_dim(outgoing, lax.axis_index("dp") * share, share, 2)
     arrived = lax.all_to_all(outgoing, "row", split_axis=0, concat_axis=0, tiled=True)
     matrix = arrived.reshape(feature_count, share)
-    gram = lax.psum(product(matrix, matrix, True).astype(low), ("dp", "col")).astype(jnp.float32)
+    gram = _group_steps_all(product(matrix, matrix, True).astype(low), ("dp", "col")).astype(
+        jnp.float32
+    )
     factor, scale, gram_norm = polynomial_factor(gram)
     ortho = (scale * matrix.astype(jnp.float32) + matrix_product(factor, matrix)) * lax.rsqrt(
         gram_norm

time: 444 us -> 472 us (1.063)
  waiting for transfers between devices: 92.2 us -> 120 us
    all_gather x0 -> x1, waiting for transfers between devices: none -> 83.8 us  [_group_steps_all(): wide_out = lax.all_gather(payload, ax_name)]
    psum x1 -> x0, waiting for transfers between devices: 50.5 us -> none  [local(): lax.psum(product(matrix, matrix, True).astype(low), ('dp', 'col'))]
    reduce_scatter x1, waiting for transfers between devices: 11 us -> 2.17 us  [local(): lax.psum_scatter(product(grad_qkv_low, w_qkv, True).astype(low), 'col', s...]
    reduce_sum x0 -> x1, other arithmetic: none -> 5.71 us  [_group_steps_all(): reply = jnp.sum(wide_out, axis=0)]
    unnamed x105 -> x113, local copies, waits for them, and re-layouts: 16.8 us -> 14.7 us
  transfers between devices with their start and end apart: 10 -> 10, of which waited for: 5 -> 5; matrix products, arithmetic and copies ran while one was open for 17% -> 16% of each run, Pallas kernels for 0% -> 0%
where the time goes in v1:
time: 472 us; the launch traced here: 471 us
  blocking collectives  213 us (45%)
  waiting for transfers between devices  120 us (25%)
  matrix products  49.7 us (11%)
  other arithmetic  34.7 us (7%)
  local copies, waits for them, and re-layouts  33.6 us (7%)
  between operations  15.2 us (3%)
    all_gather x3, blocking collectives, gather_grid(): blocks = lax.all_gather(local_piece, ('col', 'row'), axis=0, tiled=False)  136 us
    all_gather x1, waiting for transfers between devices, _group_steps_all(): wide_out = lax.all_gather(payload, ax_name)  83.8 us
    all_gather x1, blocking collectives, local(): attn_all = lax.all_gather(attn_local, 'col', axis=1, tiled=True)  16.6 us
    dot_general x5, matrix products, matrix_product(): jnp.dot(left_side.astype(jnp.bfloat16), right_side.astype(jnp.bfloat16),...  15.5 us
    psum x1, waiting for transfers between devices, local(): lax.psum(block.astype(low), 'dp').astype(jnp.float32)  15.3 us
    unnamed x113, local copies, waits for them, and re-layouts  14.7 us
    psum x1, blocking collectives, local(): grad_rows = lax.psum(row_terms, ('dp', 'col'))  14.5 us
    all_to_all x1, blocking collectives, local(): lax.all_to_all(outgoing, 'row', split_axis=0, concat_axis=0, tiled=True)  13.6 us
  transfers between devices with their start and end apart: 10, of which 5 were waited for; matrix products, arithmetic and copies ran while one was open for 16% of the time, Pallas kernels for 0%

profile of v1, /device:TPU:0, one launch (start us, length us, event | category | flops | bytes accessed | tf_op | source)
XLA Modules:
  0.0 470.9 jit_solution(6001297975162511623)
XLA Ops:
  9.5 47.6 %all-gather = bf16[2048,192]{0,1:T(8,128)(2,1)S(1)} all-gather(bf16[128,192]{0,1:T(8,128)(2,1)} %param.17), channel_id=2, replica_groups=mesh['dp'=2,'row'=4,'col'=4] {'col','row'}, dimensions={0}, use_global_device_ids=true | all-gather | bytes 835584 | tf_op jit(solution)/shard_map/all_gather | solution.py:55
  60.2 6.9 %all-gather.5 = f32[4,192,6]{1,2,0:T(8,128)S(1)} all-gather(f32[1,192,6]{1,2,0:T(8,128)S(1)} %bitcast.211), channel_id=1, replica_groups=mesh['dp'=2,'row'=4,'col'=4] {'row'}, dimensions={0}, use_global_device_ids=true | all-gather | bytes 23040 | tf_op jit(solution)/shard_map/all_gather | solution.py:136
  69.0 13.3 %all_gather.51 = bf16[768,576]{1,0:T(8,128)(2,1)S(1)} all-gather(bf16[192,576]{1,0:T(8,128)(2,1)S(1)} %copy-done.18), channel_id=1, replica_groups=mesh['dp'=2,'row'=4,'col'=4] {'row'}, dimensions={0}, use_global_device_ids=true | all-gather | bytes 1105920 | tf_op jit(solution)/shard_map/all_gather | solution.py:135
  85.5 43.6 %all-gather.2 = bf16[2048,192]{0,1:T(8,128)(2,1)S(1)} all-gather(bf16[128,192]{0,1:T(8,128)(2,1)S(1)} %copy-done.33), channel_id=4, replica_groups=mesh['dp'=2,'row'=4,'col'=4] {'col','row'}, dimensions={0}, use_global_device_ids=true | all-gather | bytes 835584 | tf_op jit(solution)/shard_map/all_gather | solution.py:55
  131.5 4.1 fusion.73
  139.4 16.6 %all_gather.52 = bf16[512,768]{0,1:T(8,128)(2,1)} all-gather(bf16[512,192]{0,1:T(8,128)(2,1)S(1)} %bitcast.197), channel_id=1, replica_groups=mesh['dp'=2,'row'=4,'col'=4] {'col'}, dimensions={1}, use_global_device_ids=true | all-gather | bytes 983040 | tf_op jit(solution)/shard_map/all_gather | solution.py:170
  156.0 3.8 copy.219
  159.8 3.1 reshape.253
  162.9 2.6 fusion.70
  168.0 3.8 multiply_convert_fusion.1
  171.8 4.2 convert_reduce_fusion
  182.6 12.3 %reduce-scatter.12.cloned.1.call-done = bf16[128,192]{1,0:T(8,128)(2,1)} async-done(((bf16[512,192]{1,0:T(8,128)(2,1)}), bf16[128,192]{1,0:T(8,128)(2,1)}) %reduce-scatter.12.cloned.1.call-update) | async-done | bytes 49168 | tf_op jit(solution)/shard_map/reduce_scatter | solution.py:179
  195.9 44.8 %all-gather.3 = bf16[2048,192]{0,1:T(8,128)(2,1)} all-gather(bf16[128,192]{0,1:T(8,128)(2,1)S(1)} %copy.201), channel_id=5, replica_groups=mesh['dp'=2,'row'=4,'col'=4] {'col','row'}, dimensions={0}, use_global_device_ids=true | all-gather | bytes 835584 | tf_op jit(solution)/shard_map/all_gather | solution.py:55
  244.6 3.0 copy.174
  260.4 15.3 %all-reduce.7.cloned.1.call-done = (bf16[192,192]{0,1:T(8,128)(2,1)}, bf16[192,576]{1,0:T(8,128)(2,1)}, bf16[192,768]{1,0:T(8,128)(2,1)}, bf16[768,192]{0,1:T(8,128)(2,1)}) async-done(((bf16[192,192]{0,1:T(8,128)(2,1)}, bf16[192,576]{1,0:T(8,128)(2,1)}, bf16[192,768]{1,0:T(8,128)(2,1)}, bf16[768,192]{0,1:T(8,128)(2,1)}), (bf16[192,192]{0,1:T(8,128)(2,1)}, bf16[192,576]{1,0:T(8,128)(2,1)}, ...) | async-done | bytes 884752 | tf_op jit(solution)/shard_map/psum | solution.py:219
  281.2 13.6 %all_to_all.10 = bf16[4,192,384]{2,1,0:T(8,128)(2,1)S(1)} all-to-all(bf16[4,192,384]{2,1,0:T(8,128)(2,1)S(1)} %fusion.34), channel_id=1, replica_groups=mesh['dp'=2,'row'=4,'col'=4] {'row'}, dimensions={0} | all-to-all | bytes 1179648 | tf_op jit(solution)/shard_map/all_to_all | solution.py:241
  303.0 83.8 %all-gather.20.cloned.1.call-done = bf16[6144,768]{1,0:T(8,128)(2,1)} async-done(((bf16[768,768]{1,0:T(8,128)(2,1)}), bf16[6144,768]{1,0:T(8,128)(2,1)}) %all-gather.20.cloned.1.call-update) | async-done | bytes 9437200 | tf_op jit(solution)/shard_map/all_gather | solution.py:20
  386.7 5.7 %reduce_sum.204 = bf16[768,768]{1,0:T(8,128)(2,1)S(1)} reduce(bf16[8,768,768]{2,1,0:T(8,128)(2,1)} %bitcast.183, bf16[]{:T(256)} %constant.27.clone.1), dimensions={0}, to_apply=%region_31.32 | reduce | flops 4128768 | bytes 10616834 | tf_op jit(solution)/shard_map/reduce_sum | solution.py:21
  397.0 2.9 multiply_add_fusion.3
  403.6 6.3 %fusion.18 = bf16[768,384]{1,0:T(8,128)(2,1)} fusion(bf16[768,384]{1,0:T(8,128)(2,1)S(1)} %bitcast.190, f32[768,768]{1,0:T(8,128)} %multiply_add_fusion.4, f32[768,768]{1,0:T(8,128)} %multiply_add_fusion.1, f32[]{:T(128)S(6)} %rsqrt.28), kind=kOutput, calls=%fused_computation.51 | convolution fusion | flops 1363968000 | bytes 5898244 | tf_op jit(solution)/shard_map/dot_general | solution.py:69
  409.9 3.8 all-to-all-start.1
  418.4 4.5 all-to-all-done.1
  430.2 9.8 %all-reduce.2 = (f32[128,1]{0,1:T(1,128)S(1)}, f32[128,1]{0,1:T(1,128)S(1)}) all-reduce(f32[128,1]{0,1:T(1,128)S(1)} %bitcast.223, f32[128,1]{0,1:T(1,128)S(1)} %bitcast.224), channel_id=1, replica_groups=mesh['dp'=2,'row'=4,'col'=4] {'row'}, use_global_device_ids=true, to_apply=%region_15.16 | all-reduce | flops 256 | bytes 2048 | tf_op jit(solution)/shard_map/psum | solution.py:277
  442.1 14.5 %psum.71 = f32[6,192]{1,0:T(8,128)S(1)} all-reduce(f32[6,192]{1,0:T(8,128)S(1)} %stack.58), channel_id=1, replica_groups=mesh['dp'=2,'row'=4,'col'=4] {'dp','col'}, use_global_device_ids=true, to_apply=%region_30.31 | all-reduce | flops 1152 | bytes 9216 | tf_op jit(solution)/shard_map/psum | solution.py:297
  (211 shorter events, 85.8 us)
Async XLA Ops:
  7.2 148.8 %all-gather.18.cloned.1.call-start = ((), (), s32[]{:S(2)}) async-start(), calls=%async_computation.8 | async-start | bytes 1671168 | tf_op jit(solution)/shard_map/all_gather | solution.py:55
  7.9 160.1 %all-gather.12.cloned.1.call-start = ((), (), s32[]{:S(2)}) async-start(), calls=%async_computation.5 | async-start | bytes 1474560 | tf_op jit(solution)/shard_map/all_gather | solution.py:138
  8.7 163.1 %all-gather.14.cloned.1.call-start = ((), (), s32[]{:S(2)}) async-start(), calls=%async_computation.6 | async-start | bytes 1474560 | tf_op jit(solution)/shard_map/all_gather | solution.py:141
  9.4 185.5 %reduce-scatter.12.cloned.1.call-start = ((), (), s32[]{:S(2)}) async-start(), calls=%async_computation.11 | async-start | bytes 327680 | tf_op jit(solution)/shard_map/reduce_scatter | solution.py:179
  137.9 21.9 %copy-start.1 = (bf16[3,512,512]{1,2,0:T(8,128)(2,1)}, bf16[3,512,512]{1,2,0:T(8,128)(2,1)S(1)}, u32[]{:S(2)}) copy-start(bf16[3,512,512]{1,2,0:T(8,128)(2,1)S(1)} %fusion.19) | copy-start | bytes 4718596
  178.2 97.5 %all-reduce.7.cloned.1.call-start = ((), (), s32[]{:S(2)}) async-start(), calls=%async_computation.13 | async-start | bytes 1867776 | tf_op jit(solution)/shard_map/psum | solution.py:219
  260.1 17.7 %copy-start.25 = (f32[192,768]{1,0:T(8,128)S(1)}, f32[192,768]{1,0:T(8,128)}, u32[]{:S(2)}) copy-start(f32[192,768]{1,0:T(8,128)} %param.29) | copy-start | bytes 1769476
  260.2 126.6 %all-gather.20.cloned.1.call-start = ((), (), s32[]{:S(2)}) async-start(), calls=%async_computation.9 | async-start | bytes 10616832 | tf_op jit(solution)/shard_map/all_gather | solution.py:20
  296.6 120.7 %reduce-scatter.10.cloned.1.call-start = ((), (), s32[]{:S(2)}) async-start(), calls=%async_computation.10 | async-start | bytes 327680 | tf_op jit(solution)/shard_map/reduce_scatter | solution.py:268
  300.5 128.6 %reduce-scatter.14.cloned.1.call-start = ((), (), s32[]{:S(2)}) async-start(), calls=%async_computation.12 | async-start | bytes 327680 | tf_op jit(solution)/shard_map/reduce_scatter | solution.py:272
  409.9 13.9 %copy-start.41 = (f32[576]{0:T(1024)S(1)}, f32[576]{0:T(1024)}, u32[]{:S(2)}) copy-start(f32[576]{0:T(1024)} %param.24) | copy-start | bytes 6916
  409.9 13.9 %copy-start.42 = (f32[576]{0:T(1024)S(1)}, f32[576]{0:T(1024)}, u32[]{:S(2)}) copy-start(f32[576]{0:T(1024)} %param.31) | copy-start | bytes 6916
  409.9 16.3 %copy-start.32 = (bf16[128,192]{1,0:T(8,128)(2,1)S(1)}, bf16[128,192]{1,0:T(8,128)(2,1)}, u32[]{:S(2)}) copy-start(bf16[128,192]{1,0:T(8,128)(2,1)} %reduce-scatter.12.cloned.1.call-done) | copy-start | bytes 147460
  409.9 16.4 %copy-start.44 = (f32[768]{0:T(1024)S(1)}, f32[768]{0:T(1024)}, u32[]{:S(2)}) copy-start(f32[768]{0:T(1024)} %param.25) | copy-start | bytes 9220
  409.9 16.4 %copy-start.45 = (f32[768]{0:T(1024)S(1)}, f32[768]{0:T(1024)}, u32[]{:S(2)}) copy-start(f32[768]{0:T(1024)} %param.32) | copy-start | bytes 9220
  409.9 46.7 %copy-start.39 = (f32[6,192]{1,0:T(8,128)S(1)}, f32[6,192]{1,0:T(8,128)}, u32[]{:S(2)}) copy-start(f32[6,192]{1,0:T(8,128)} %param.33) | copy-start | bytes 13828
  409.9 13.0 %all-to-all-start.1 = ((bf16[4,192,384]{2,1,0:T(8,128)(2,1)}), bf16[4,192,384]{2,1,0:T(8,128)(2,1)S(1)}, u32[]{:S(2)}, u32[]{:S(2)}) async-start(bf16[4,192,384]{2,1,0:T(8,128)(2,1)} %bitcast.51), calls=%async_computation.1 | async-start | bytes 1179648 | tf_op jit(solution)/shard_map/all_to_all | solution.py:250
  413.7 43.6 %copy-start.29 = (bf16[192,192]{0,1:T(8,128)(2,1)S(1)}, bf16[192,192]{0,1:T(8,128)(2,1)}, u32[]{:S(2)}) copy-start(bf16[192,192]{0,1:T(8,128)(2,1)} %get-tuple-element.180) | copy-start | bytes 221188
  413.7 44.4 %copy-start.23 = (f32[192,192]{0,1:T(8,128)S(1)}, f32[192,192]{0,1:T(8,128)}, u32[]{:S(2)}) copy-start(f32[192,192]{0,1:T(8,128)} %get-tuple-element.207) | copy-start | bytes 442372
  413.7 45.2 %all-gather.16.cloned.1.call-start = ((), (), s32[]{:S(2)}) async-start(), calls=%async_computation.7 | async-start | bytes 1769472 | tf_op jit(solution)/shard_map/all_gather | solution.py:257
  417.3 42.6 %copy-start.46 = (f32[576]{0:T(1024)}, f32[576]{0:T(1024)S(1)}, u32[]{:S(2)}) copy-start(f32[576]{0:T(1024)S(1)} %get-tuple-element.178) | copy-start | bytes 6916
  417.3 42.6 %copy-start.47 = (f32[768]{0:T(1024)}, f32[768]{0:T(1024)S(1)}, u32[]{:S(2)}) copy-start(f32[768]{0:T(1024)S(1)} %get-tuple-element.179) | copy-start | bytes 9220
  423.8 36.9 %copy-start.19 = (bf16[192,576]{1,0:T(8,128)(2,1)S(1)}, bf16[192,576]{1,0:T(8,128)(2,1)}, u32[]{:S(2)}) copy-start(bf16[192,576]{1,0:T(8,128)(2,1)} %param.20) | copy-start | bytes 663556
  440.1 22.5 %copy-start.13 = (bf16[192,768]{1,0:T(8,128)(2,1)S(1)}, bf16[192,768]{1,0:T(8,128)(2,1)}, u32[]{:S(2)}) copy-start(bf16[192,768]{1,0:T(8,128)(2,1)} %param.22) | copy-start | bytes 884740
  (35 other events, 118.4 us)
Sparse Core Ops, SparseCore 0:
  10.8 64.3 all-gather.17
  77.0 32.7 all-gather.11
  111.6 27.0 all-gather.13
  178.3 16.5 reduce-scatter.11
  260.3 15.2 all-reduce.6
  296.7 89.9 all-gather.19
  389.6 18.3 reduce-scatter.9
  410.8 18.2 reduce-scatter.13
  431.2 7.3 all-gather.15
